TPU v7x, 32 devices: a whole 2x2x4 slice. The times are simulated.
32 devices in a mesh: leaf: 8 (over z, y), rows: 4 (over x, core).
Axes of the slice: x: 2, y: 2, z: 4, core: 2. Of those that a mesh axis runs over, the one named last changes fastest.
Arguments:
- sigma_top: float32 [2048, 1024], P('leaf'), may hold values from -4 to 40, as said below
- panel_top: float32 [1024, 12288], P(None, 'leaf'), may hold values from -0.125 to 0.125
- diag_top: float32 [12288, 256], P('leaf'), may hold values from -4 to 20, as said below
- panel_mid: float32 [1024, 24576], P(None, ('leaf', 'rows')), may hold values from -0.125 to 0.125
- diag_mid: float32 [24576, 256], P(('leaf', 'rows')), may hold values from -4 to 20, as said below
- pattern_mid: int32 [4, 4], replicated, may hold values from 0 to 23, as said below
- panel_low: float32 [1024, 49152], P(None, ('leaf', 'rows')), may hold values from -0.125 to 0.125
- diag_low: float32 [49152, 256], P(('leaf', 'rows')), may hold values from -4 to 20, as said below
- pattern_low: int32 [8, 4], replicated, may hold values from 0 to 23, as said below
Outputs:
- cross_top: float32 [1024, 12288], P('rows', 'leaf')
- marginal_top: float32 [12288, 256], P(('leaf', 'rows'))
- cross_mid: float32 [1024, 24576], P(None, ('leaf', 'rows'))
- marginal_mid: float32 [24576, 256], P(('leaf', 'rows'))
- cross_low: float32 [1024, 49152], P(None, ('leaf', 'rows'))
- marginal_low: float32 [49152, 256], P(('leaf', 'rows'))
Inputs may be any that keep to these rules, and one draw needn't show every extreme that they name: Each block of 1024 rows of sigma_top is symmetric. `diag_top`: each 256 x 256 block is symmetric. `diag_mid`: each block of 256 rows is symmetric. `diag_low`: each block of 256 rows is symmetric. `pattern_mid`: the 4 entries of a row are different; rows 2i and 2i + 1 together name 8 different blocks. `pattern_low`: the 4 entries of a row are different; rows 2i and 2i + 1 together name 8 different blocks.
All inputs are finite; a program needn't handle non-finite values.
Results may differ from a plain program's by a relative error of at most 0.00009.
Values sent between devices are 32-bit elements; how exact they have to be, the bound alone decides.
A program may use at most 192 MiB of HBM per device.

v0:
```python
import jax
import jax.numpy as jnp
from jax import lax
from jax.sharding import PartitionSpec as P

HIGH = lax.Precision.HIGHEST


def from_partner(value, axis, bit):
    return lax.ppermute(value, axis, [(i, i ^ 1 << bit) for i in range(lax.axis_size(axis))])


def block_diagonal(blocks):
    block_count = blocks.shape[0]
    block_side = blocks.shape[1]
    eye_table = jnp.eye(block_count, dtype=blocks.dtype)
    spread_out = blocks[:, :, None, :] * eye_table[:, None, :, None]
    return spread_out.reshape(block_count * block_side, block_count * block_side)


def select_blocks(panel_cols, diag_blocks, wanted, owned_mask, block_size):
    rows_total = panel_cols.shape[0]
    local_count = panel_cols.shape[1] // block_size
    taken_blocks = (
        jnp.take(panel_cols.reshape(rows_total, local_count, block_size), wanted, axis=1)
        * owned_mask[None, :, None]
    )
    taken_diag = (
        jnp.take(diag_blocks.reshape(local_count, block_size, block_size), wanted, axis=0)
        * owned_mask[:, None, None]
    )
    return (taken_blocks.reshape(rows_total, -1), taken_diag.reshape(-1, block_size))


def child_cov(parent_cov, chosen, chosen_diag, block_size):
    block_count = chosen_diag.shape[0] // block_size
    product = jnp.dot(parent_cov, chosen, precision=HIGH, preferred_element_type=jnp.float32)
    inner_part = jnp.dot(chosen.T, product, precision=HIGH, preferred_element_type=jnp.float32)
    return inner_part + block_diagonal(chosen_diag.reshape(block_count, block_size, block_size))


def marg_terms(panel_cols, cover_cols, block_size):
    rows_total = panel_cols.shape[0]
    block_count = panel_cols.shape[1] // block_size
    terms = jnp.einsum(
        "sai,saj->aij",
        panel_cols.reshape(rows_total, block_count, block_size),
        cover_cols.reshape(rows_total, block_count, block_size),
        precision=HIGH,
    )
    return terms.reshape(block_count * block_size, block_size)


def quad_total(pieces):
    for bit_number in range(2):
        others = from_partner((pieces[0], pieces[1], pieces[2]), "leaf", bit_number)
        pieces = (pieces[0] + others[0], pieces[1] + others[1], pieces[2] + others[2])
    return pieces


def local(
    sigma_top,
    panel_top,
    diag_top,
    panel_mid,
    diag_mid,
    pattern_mid,
    panel_low,
    diag_low,
    pattern_low,
):
    block_size = diag_top.shape[1]
    struct_rows = panel_top.shape[0]
    row_count = lax.axis_size("rows")
    leaf_index = lax.axis_index("leaf")
    rows_index = lax.axis_index("rows")
    slot_blocks = pattern_mid.shape[1]
    slot_width = slot_blocks * block_size
    quad_place = leaf_index % 4
    quad_number = leaf_index // 4
    top_local = panel_top.shape[1] // block_size
    children = 2 * quad_number + jnp.arange(2, dtype=jnp.int32)
    wanted_top = pattern_mid[children].reshape(-1)
    owned_top = (wanted_top // top_local == quad_place).astype(jnp.float32)
    chosen_top, chosen_top_diag = select_blocks(
        panel_top, diag_top, wanted_top % top_local, owned_top, block_size
    )
    padded_cov = lax.dynamic_update_slice_in_dim(
        jnp.zeros((struct_rows, struct_rows), jnp.float32),
        sigma_top,
        quad_place * sigma_top.shape[0],
        0,
    )
    share_rows = struct_rows // row_count
    diag_share = chosen_top_diag.shape[0] // row_count
    pieces = (
        lax.dynamic_slice_in_dim(padded_cov, rows_index * share_rows, share_rows, 0),
        lax.dynamic_slice_in_dim(chosen_top, rows_index * share_rows, share_rows, 0),
        lax.dynamic_slice_in_dim(chosen_top_diag, rows_index * diag_share, diag_share, 0),
    )
    pieces = quad_total(pieces)
    parent_cov, chosen_all, chosen_diag_all = (
        lax.all_gather(pieces[0], "rows", axis=0, tiled=True),
        lax.all_gather(pieces[1], "rows", axis=0, tiled=True),
        lax.all_gather(pieces[2], "rows", axis=0, tiled=True),
    )
    mid_local = panel_mid.shape[1] // block_size
    pair_number = leaf_index // 2
    pair_place = leaf_index % 2 * row_count + rows_index
    low_children = 2 * pair_number + jnp.arange(2, dtype=jnp.int32)
    wanted_mid = pattern_low[low_children].reshape(-1)
    owned_mid = (wanted_mid // mid_local == pair_place).astype(jnp.float32)
    chosen_mid, chosen_mid_diag = select_blocks(
        panel_mid, diag_mid, wanted_mid % mid_local, owned_mid, block_size
    )
    summed = lax.psum((chosen_mid, chosen_mid_diag), "rows")
    partner = from_partner((summed[0], summed[1]), "leaf", 0)
    mid_all = summed[0] + partner[0]
    mid_diag_all = summed[1] + partner[1]
    share_struct = struct_rows // row_count
    cov_rows = lax.dynamic_slice_in_dim(parent_cov, rows_index * share_struct, share_struct, 0)
    cross_top = -jnp.dot(cov_rows, panel_top, precision=HIGH, preferred_element_type=jnp.float32)
    panel_rows = lax.dynamic_slice_in_dim(panel_top, rows_index * share_struct, share_struct, 0)
    partial_value = marg_terms(panel_rows, cross_top, block_size)
    piece_rows = partial_value.shape[0] // row_count
    own_diag = lax.dynamic_slice_in_dim(diag_top, rows_index * piece_rows, piece_rows, 0)
    summed_terms = lax.psum(partial_value, "rows")
    marginal_top = own_diag - lax.dynamic_slice_in_dim(
        summed_terms, rows_index * piece_rows, piece_rows, 0
    )
    child_place = leaf_index // 2 % 2
    own_slots = lax.dynamic_slice_in_dim(chosen_all, child_place * slot_width, slot_width, 1)
    own_slot_diag = lax.dynamic_slice_in_dim(
        chosen_diag_all, child_place * slot_width, slot_width, 0
    )
    mid_cov = child_cov(parent_cov, own_slots, own_slot_diag, block_size)
    cross_mid = -jnp.dot(mid_cov, panel_mid, precision=HIGH, preferred_element_type=jnp.float32)
    marginal_mid = diag_mid - marg_terms(panel_mid, cross_mid, block_size)
    low_place = leaf_index % 2
    low_slots = lax.dynamic_slice_in_dim(mid_all, low_place * slot_width, slot_width, 1)
    low_slot_diag = lax.dynamic_slice_in_dim(mid_diag_all, low_place * slot_width, slot_width, 0)
    low_cov = child_cov(mid_cov, low_slots, low_slot_diag, block_size)
    cross_low = -jnp.dot(low_cov, panel_low, precision=HIGH, preferred_element_type=jnp.float32)
    marginal_low = diag_low - marg_terms(panel_low, cross_low, block_size)
    return (cross_top, marginal_top, cross_mid, marginal_mid, cross_low, marginal_low)


def solution(mesh):
    return jax.shard_map(
        local,
        mesh=mesh,
        in_specs=(
            P("leaf", None),
            P(None, "leaf"),
            P("leaf", None),
            P(None, ("leaf", "rows")),
            P(("leaf", "rows"), None),
            P(),
            P(None, ("leaf", "rows")),
            P(("leaf", "rows"), None),
            P(),
        ),
        out_specs=(
            P("rows", "leaf"),
            P(("leaf", "rows"), None),
            P(None, ("leaf", "rows")),
            P(("leaf", "rows"), None),
            P(None, ("leaf", "rows")),
            P(("leaf", "rows"), None),
        ),
        check_vma=False,
    )
```

profile of v0, /device:TPU:0, one launch (start us, length us, event | category | flops | bytes accessed | tf_op | source)
XLA Modules:
  0.0 711.9 jit_solution(2259707078649836408)
XLA Ops:
  8.6 3.1 collective-permute-start
  11.7 23.2 %collective-permute-done = f32[256,1024]{1,0:T(8,128)S(1)} collective-permute-done((f32[256,1024]{1,0:T(8,128)S(1)}, f32[256,1024]{1,0:T(8,128)S(1)}, u32[]{:S(2)}, u32[]{:S(2)}) %collective-permute-start) | collective-permute-done | bytes 1048608 | tf_op jit(solution)/shard_map/ppermute | solution.py:10
  36.9 22.5 %collective-permute-done.1 = f32[256,1024]{1,0:T(8,128)S(1)} collective-permute-done((f32[256,1024]{1,0:T(8,128)S(1)}, f32[256,1024]{1,0:T(8,128)S(1)}, u32[]{:S(2)}, u32[]{:S(2)}) %collective-permute-start.1) | collective-permute-done | bytes 1048608 | tf_op jit(solution)/shard_map/ppermute | solution.py:10
  66.2 5.1 gather_fusion.4
  71.3 9.2 %copy.46 = f32[1024,8,256]{0,2,1:T(8,128)} copy(f32[1024,8,256]{2,0,1:T(8,128)} %bitcast.66) | data formatting | bytes 16777216 | tf_op jit(solution)/shard_map/jit(_take)/gather | solution.py:25
  86.5 5.9 fusion
  92.4 3.9 all-gather.4.cloned.1.call-done
  96.4 7.9 %convolution_negate_fusion.1 = f32[256,1536]{1,0:T(8,128)S(1)} fusion(f32[1024,1536]{1,0:T(8,128)} %param.10, f32[1024,1024]{1,0:T(8,128)} %all-gather.4.cloned.1.call-done, s32[]{:T(128)S(6)} %select_n.181), kind=kOutput, calls=%fused_computation.15 | convolution fusion | flops 4832231424 | bytes 8912900 | tf_op jit(solution)/shard_map/dot_general | solution.py:122
  105.9 4.2 fusion.25
  110.5 6.6 copy.39
  117.8 6.6 copy.40
  124.4 7.1 %gather_fusion.1 = f32[8,1024,256]{2,1,0:T(8,128)} fusion(f32[1024,6,256]{2,0,1:T(8,128)} %copy.40, s32[1024]{0:T(1024)S(1)} %pad_clamp_fusion.2), kind=kCustom, calls=%fused_computation.1 | custom fusion | bytes 16777248 | tf_op jit(solution)/shard_map/jit(_take)/gather | solution.py:25
  131.5 9.2 %copy.41 = f32[1024,8,256]{0,2,1:T(8,128)} copy(f32[1024,8,256]{2,0,1:T(8,128)} %bitcast.67) | data formatting | bytes 16777216 | tf_op jit(solution)/shard_map/jit(_take)/gather | solution.py:25
  148.6 54.6 %collective-permute-done.4 = f32[512,256]{1,0:T(8,128)S(1)} collective-permute-done((f32[512,256]{1,0:T(8,128)S(1)}, f32[512,256]{1,0:T(8,128)S(1)}, u32[]{:S(2)}, u32[]{:S(2)}) %collective-permute-start.4) | collective-permute-done | bytes 524320 | tf_op jit(solution)/shard_map/ppermute | solution.py:10
  205.1 11.6 %collective-permute-done.5 = f32[512,256]{1,0:T(8,128)S(1)} collective-permute-done((f32[512,256]{1,0:T(8,128)S(1)}, f32[512,256]{1,0:T(8,128)S(1)}, u32[]{:S(2)}, u32[]{:S(2)}) %collective-permute-start.5) | collective-permute-done | bytes 524320 | tf_op jit(solution)/shard_map/ppermute | solution.py:10
  221.9 44.5 %collective-permute-done.3 = f32[256,2048]{0,1:T(8,128)S(1)} collective-permute-done((f32[256,2048]{0,1:T(8,128)S(1)}, f32[256,2048]{0,1:T(8,128)S(1)}, u32[]{:S(2)}, u32[]{:S(2)}) %collective-permute-start.3) | collective-permute-done | bytes 2097184 | tf_op jit(solution)/shard_map/ppermute | solution.py:10
  268.1 54.4 %all-reduce.3.cloned.1.call-done = (f32[1536,256]{1,0:T(8,128)}, f32[1024,2048]{0,1:T(8,128)}, f32[2048,256]{1,0:T(8,128)}) async-done(((f32[1536,256]{1,0:T(8,128)}, f32[1024,2048]{0,1:T(8,128)}, f32[2048,256]{1,0:T(8,128)}), (f32[1536,256]{1,0:T(8,128)}, f32[1024,2048]{0,1:T(8,128)}, f32[2048,256]{1,0:T(8,128)})) %all-reduce.3.cloned.1.call-update) | async-done | bytes 12058640 | tf_op jit(solution)/shard_map/psum | solution.py:127
  324.5 6.7 copy.48
  331.2 16.3 %all-gather.8.cloned.1.call-done = f32[2048,256]{1,0:T(8,128)} async-done(((f32[512,256]{1,0:T(8,128)}), f32[2048,256]{1,0:T(8,128)}) %all-gather.8.cloned.1.call-update) | async-done | bytes 2097168 | tf_op jit(solution)/shard_map/all_gather | solution.py:105
  350.7 198.7 %collective-permute-done.7 = f32[2048,256]{1,0:T(8,128)} collective-permute-done((f32[2048,256]{1,0:T(8,128)}, f32[2048,256]{1,0:T(8,128)}, u32[]{:S(2)}, u32[]{:S(2)}) %collective-permute-start.7) | collective-permute-done | bytes 2097184 | tf_op jit(solution)/shard_map/ppermute | solution.py:10
  552.5 3.0 copy.55
  555.5 3.0 copy.57
  558.5 25.9 %fusion.4 = f32[1024,1024]{1,0:T(8,128)S(1)} fusion(f32[1024,1024]{1,0:T(8,128)} %all-gather.4.cloned.1.call-done, f32[1024,2048]{0,1:T(8,128)} %all-gather.6.cloned.1.call-done, s32[]{:T(128)S(6)} %select_n.193), kind=kOutput, calls=%fused_computation.13 | convolution fusion | flops 12884901888 | bytes 12582916 | tf_op jit(solution)/shard_map/dot_general | solution.py:37
  584.4 14.0 %fusion.8 = f32[1024,1024]{1,0:T(8,128)S(1)} fusion(f32[1024,1024]{1,0:T(8,128)S(1)} %bitcast.75, f32[1024,1024]{1,0:T(8,128)S(1)} %fusion.4, f32[1024,2048]{0,1:T(8,128)S(1)} %copy-done.13, s32[]{:T(128)S(6)} %select_n.193), kind=kOutput, calls=%fused_computation.22 | convolution fusion | flops 12885950464 | bytes 16777220 | tf_op jit(solution)/shard_map/dot_general | solution.py:38
  600.4 12.4 %convolution_negate_fusion.2 = f32[1024,768]{0,1:T(8,128)} fusion(f32[1024,1024]{1,0:T(8,128)S(1)} %fusion.8, f32[1024,768]{1,0:T(8,128)S(1)} %copy-done.12), kind=kOutput, calls=%fused_computation.23 | convolution fusion | flops 9664462848 | bytes 10485760 | tf_op jit(solution)/shard_map/dot_general | solution.py:137
  612.8 4.1 copy.50
  616.9 5.3 fusion.26
  623.3 17.4 %fusion.11 = f32[1024,1024]{1,0:T(8,128)S(1)} fusion(f32[1024,1024]{1,0:T(8,128)S(1)} %copy-done.4, f32[1024,2048]{0,1:T(8,128)} %collective-permute-done.6, s32[]{:T(128)S(6)} %select_n.204, f32[1024,2048]{0,1:T(8,128)} %get-tuple-element.25), kind=kOutput, calls=%fused_computation.25 | convolution fusion | flops 12885950464 | bytes 16777220 | tf_op jit(solution)/shard_map/dot_general | solution.py:37
  640.8 16.3 %fusion.12 = f32[1024,1024]{1,0:T(8,128)S(1)} fusion(f32[1024,1024]{1,0:T(8,128)S(1)} %fusion.11, f32[1024,2048]{0,1:T(8,128)} %collective-permute-done.6, s32[]{:T(128)S(6)} %select_n.204, f32[1024,2048]{0,1:T(8,128)S(1)} %bitcast.81), kind=kOutput, calls=%fused_computation.26 | convolution fusion | flops 12885950464 | bytes 16777220 | tf_op jit(solution)/shard_map/dot_general | solution.py:38
  657.1 22.3 %convolution_negate_fusion = f32[1024,1536]{1,0:T(8,128)} fusion(f32[1024,1536]{1,0:T(8,128)S(1)} %bitcast.83, f32[1024,1024]{1,0:T(8,128)S(1)} %fusion.12, f32[1024,1024]{1,0:T(8,128)S(1)} %bitcast.89), kind=kOutput, calls=%fused_computation.8 | convolution fusion | flops 19329974272 | bytes 20971520 | tf_op jit(solution)/shard_map/dot_general | solution.py:143
  679.4 6.6 copy.47
  686.0 17.6 %fusion.27 = f32[6,256,256]{1,2,0:T(8,128)S(1)} fusion(f32[1024,6,256]{0,2,1:T(8,128)} %bitcast.72, f32[1024,6,256]{0,2,1:T(8,128)} %bitcast.70), kind=kOutput, calls=%fused_computation.78 | convolution fusion | flops 4831838208 | bytes 14155776 | tf_op jit(solution)/shard_map/sai,saj->aij/dot_general | solution.py:45
  (124 shorter events, 48.1 us)
Async XLA Ops:
  7.2 109.9 %copy-start = (s32[4,4]{1,0:T(4,128)S(1)}, s32[4,4]{1,0:T(4,128)}, u32[]{:S(2)}) copy-start(s32[4,4]{1,0:T(4,128)} %param.14) | copy-start | bytes 196
  7.2 89.2 %all-gather.4.cloned.1.call-start = ((), (), s32[]{:S(2)}) async-start(), calls=%async_computation | async-start | bytes 5242880 | tf_op jit(solution)/shard_map/all_gather | solution.py:103
  8.6 52.0 %copy-start.17 = (s32[8,4]{0,1:T(4,128)S(1)}, s32[8,4]{0,1:T(4,128)}, u32[]{:S(2)}) copy-start(s32[8,4]{0,1:T(4,128)} %param.17) | copy-start | bytes 388
  8.6 52.9 %copy-start.11 = (f32[1024,768]{1,0:T(8,128)S(1)}, f32[1024,768]{1,0:T(8,128)}, u32[]{:S(2)}) copy-start(f32[1024,768]{1,0:T(8,128)} %param.12) | copy-start | bytes 9437188
  8.6 26.2 %collective-permute-start = (f32[256,1024]{1,0:T(8,128)S(1)}, f32[256,1024]{1,0:T(8,128)S(1)}, u32[]{:S(2)}, u32[]{:S(2)}) collective-permute-start(f32[256,1024]{1,0:T(8,128)S(1)} %constant_dynamic-slice_fusion.2), channel_id=1, source_target_pairs={{0,4},{4,0},{8,12},{12,8},{16,20},{20,16},{24,28},{28,24},{1,5},{5... | collective-permute-start | bytes 3145736 | tf_op jit(solution)/shard_map/ppermute | solution.py:10
  35.0 24.4 %collective-permute-start.1 = (f32[256,1024]{1,0:T(8,128)S(1)}, f32[256,1024]{1,0:T(8,128)S(1)}, u32[]{:S(2)}, u32[]{:S(2)}) collective-permute-start(f32[256,1024]{1,0:T(8,128)S(1)} %fusion.44), channel_id=1, source_target_pairs={{0,8},{4,12},{8,0},{12,4},{16,24},{20,28},{24,16},{28,20},{1,9},{5... | collective-permute-start | bytes 3145736 | tf_op jit(solution)/shard_map/ppermute | solution.py:10
  60.6 261.9 %all-reduce.3.cloned.1.call-start = ((), (), s32[]{:S(2)}) async-start(), calls=%async_computation.3 | async-start | bytes 24117248 | tf_op jit(solution)/shard_map/psum | solution.py:127
  80.5 3.5 copy-start.6
  92.4 13.5 %copy-start.9 = (f32[256,1536]{0,1:T(8,128)S(1)}, f32[256,1536]{0,1:T(8,128)}, u32[]{:S(2)}) copy-start(f32[256,1536]{0,1:T(8,128)} %copy.36) | copy-start | bytes 4718596
  104.3 5.9 copy-start.8
  110.2 237.4 %all-gather.8.cloned.1.call-start = ((), (), s32[]{:S(2)}) async-start(), calls=%async_computation.2 | async-start | bytes 2621440 | tf_op jit(solution)/shard_map/all_gather | solution.py:105
  144.0 73.7 %collective-permute-start.2 = (f32[256,2048]{0,1:T(8,128)}, f32[256,2048]{0,1:T(8,128)}, u32[]{:S(2)}, u32[]{:S(2)}) collective-permute-start(f32[256,2048]{0,1:T(8,128)} %fusion.6), channel_id=1, source_target_pairs={{0,4},{4,0},{8,12},{12,8},{16,20},{20,16},{24,28},{28,24},{1,5},{5... | collective-permute-start | bytes 6291464 | tf_op jit(solution)/shard_map/ppermute | solution.py:10
  148.1 55.0 %collective-permute-start.4 = (f32[512,256]{1,0:T(8,128)S(1)}, f32[512,256]{1,0:T(8,128)S(1)}, u32[]{:S(2)}, u32[]{:S(2)}) collective-permute-start(f32[512,256]{1,0:T(8,128)S(1)} %fusion.14), channel_id=1, source_target_pairs={{0,4},{4,0},{8,12},{12,8},{16,20},{20,16},{24,28},{28,24},{1,5},{5... | collective-permute-start | bytes 1572872 | tf_op jit(solution)/shard_map/ppermute | solution.py:10
  203.4 13.3 %collective-permute-start.5 = (f32[512,256]{1,0:T(8,128)S(1)}, f32[512,256]{1,0:T(8,128)S(1)}, u32[]{:S(2)}, u32[]{:S(2)}) collective-permute-start(f32[512,256]{1,0:T(8,128)S(1)} %fusion.43), channel_id=1, source_target_pairs={{0,8},{4,12},{8,0},{12,4},{16,24},{20,28},{24,16},{28,20},{1,9},{5... | collective-permute-start | bytes 1572872 | tf_op jit(solution)/shard_map/ppermute | solution.py:10
  217.6 340.9 %all-gather.6.cloned.1.call-start = ((), (), s32[]{:S(2)}) async-start(), calls=%async_computation.1 | async-start | bytes 10485760 | tf_op jit(solution)/shard_map/all_gather | solution.py:104
  220.3 46.2 %collective-permute-start.3 = (f32[256,2048]{0,1:T(8,128)S(1)}, f32[256,2048]{0,1:T(8,128)S(1)}, u32[]{:S(2)}, u32[]{:S(2)}) collective-permute-start(f32[256,2048]{0,1:T(8,128)S(1)} %fusion.42), channel_id=1, source_target_pairs={{0,8},{4,12},{8,0},{12,4},{16,24},{20,28},{24,16},{28,20},{1,9},{5... | collective-permute-start | bytes 6291464 | tf_op jit(solution)/shard_map/ppermute | solution.py:10
  322.5 300.8 %collective-permute-start.6 = (f32[1024,2048]{0,1:T(8,128)}, f32[1024,2048]{0,1:T(8,128)}, u32[]{:S(2)}, u32[]{:S(2)}) collective-permute-start(f32[1024,2048]{0,1:T(8,128)} %get-tuple-element.25), channel_id=1, source_target_pairs={{0,4},{4,0},{8,12},{12,8},{16,20},{20,16},{24,28},{28,24},{1,5},{5... | collective-permute-start | bytes 25165832 | tf_op jit(solution)/shard_map/ppermute | solution.py:10
  324.0 225.5 %collective-permute-start.7 = (f32[2048,256]{1,0:T(8,128)}, f32[2048,256]{1,0:T(8,128)}, u32[]{:S(2)}, u32[]{:S(2)}) collective-permute-start(f32[2048,256]{1,0:T(8,128)} %get-tuple-element.26), channel_id=1, source_target_pairs={{0,4},{4,0},{8,12},{12,8},{16,20},{20,16},{24,28},{28,24},{1,5},{5... | collective-permute-start | bytes 6291464 | tf_op jit(solution)/shard_map/ppermute | solution.py:10
  324.5 225.0 %copy-start.16 = (f32[2048,256]{1,0:T(8,128)S(1)}, f32[2048,256]{1,0:T(8,128)}, u32[]{:S(2)}) copy-start(f32[2048,256]{1,0:T(8,128)} %get-tuple-element.26) | copy-start | bytes 6291460
  558.5 25.9 %copy-start.5 = (f32[128,8,4,256]{3,1,2,0:T(8,128)S(1)}, f32[128,8,4,256]{3,1,2,0:T(8,128)}, u32[]{:S(2)}) copy-start(f32[128,8,4,256]{3,1,2,0:T(8,128)} %copy.55) | copy-start | bytes 12582916
  558.5 25.9 %copy-start.13 = (f32[1024,2048]{0,1:T(8,128)S(1)}, f32[1024,2048]{0,1:T(8,128)}, u32[]{:S(2)}) copy-start(f32[1024,2048]{0,1:T(8,128)} %all-gather.6.cloned.1.call-done) | copy-start | bytes 25165828
  584.4 16.0 %copy-start.12 = (f32[1024,768]{1,0:T(8,128)S(1)}, f32[1024,768]{1,0:T(8,128)}, u32[]{:S(2)}) copy-start(f32[1024,768]{1,0:T(8,128)} %param.12) | copy-start | bytes 9437188
  612.8 4.1 copy-start.2
  616.9 5.4 copy-start.7
  616.9 6.4 copy-start.4
  622.2 18.5 %slice-start = ((s8[8388608]{0:T(1024)(128)(4,1)}), s8[4194304]{0:T(1024)(128)(4,1)S(1)}, s32[]{:S(2)}) async-start(s8[8388608]{0:T(1024)(128)(4,1)} %bitcast.80), calls=%async_computation.4 | async-start | bytes 8388608
  623.3 17.4 %slice-start.1 = ((s8[8388608]{0:T(1024)(128)(4,1)}), s8[4194304]{0:T(1024)(128)(4,1)S(1)}, s32[]{:S(2)}) async-start(s8[8388608]{0:T(1024)(128)(4,1)} %bitcast.80), calls=%async_computation.5 | async-start | bytes 8388608
  623.3 33.8 %slice-start.2 = ((s8[6291456]{0:T(1024)(128)(4,1)}), s8[4194304]{0:T(1024)(128)(4,1)S(1)}, s32[]{:S(2)}) async-start(s8[6291456]{0:T(1024)(128)(4,1)} %bitcast.82), calls=%async_computation.6 | async-start | bytes 8388608
  640.7 16.3 %slice-start.3 = ((s8[6291456]{0:T(1024)(128)(4,1)}), s8[2097152]{0:T(1024)(128)(4,1)S(1)}, s32[]{:S(2)}) async-start(s8[6291456]{0:T(1024)(128)(4,1)} %bitcast.82), calls=%async_computation.7 | async-start | bytes 4194304
  640.8 16.3 %copy-start.10 = (f32[128,8,4,256]{3,1,2,0:T(8,128)S(1)}, f32[128,8,4,256]{3,1,2,0:T(8,128)}, u32[]{:S(2)}) copy-start(f32[128,8,4,256]{3,1,2,0:T(8,128)} %copy.57) | copy-start | bytes 12582916
  686.0 17.6 %copy-start.14 = (f32[1536,256]{1,0:T(8,128)S(1)}, f32[1536,256]{1,0:T(8,128)}, u32[]{:S(2)}) copy-start(f32[1536,256]{1,0:T(8,128)} %param.16) | copy-start | bytes 4718596
  686.0 18.9 %copy-start.1 = (s32[4,4]{1,0:T(4,128)S(1)}, s32[4,4]{1,0:T(4,128)}, u32[]{:S(2)}) copy-start(s32[4,4]{1,0:T(4,128)} %param.14) | copy-start | bytes 196
  (2 other events, 3.2 us)
Sparse Core Ops, SparseCore 0:
  60.7 35.6 all-gather.3
  110.3 212.1 all-reduce.2
  324.6 22.8 all-gather.7
  348.9 58.2 all-gather.5
where the time goes:
time: 720 us; the launch traced here: 712 us
  waiting for transfers between devices  430 us (60%)
  matrix products  143 us (20%)
  local copies, waits for them, and re-layouts  86.5 us (12%)
  other arithmetic  24.8 us (3%)
  between operations  14.7 us (2%)
  starting transfers between devices  12.9 us (2%)
    ppermute x8, waiting for transfers between devices, from_partner(): lax.ppermute(value, axis, [(i, i ^ 1 << bit) for i in range(lax.axis_size...  355 us
    psum x1, waiting for transfers between devices, local(): summed_terms = lax.psum(partial_value, 'rows')  54.4 us
    dot_general x2, matrix products, child_cov(): jnp.dot(parent_cov, chosen, precision=HIGH, preferred_element_type=jnp.fl...  43.3 us
    gather x4, local copies, waits for them, and re-layouts, select_blocks(): jnp.take(panel_cols.reshape(rows_total, local_count, block_size), wanted,...  30.7 us
    dot_general x2, matrix products, child_cov(): jnp.dot(chosen.T, product, precision=HIGH, preferred_element_type=jnp.flo...  30.3 us
    unnamed x55, local copies, waits for them, and re-layouts  28.7 us
    dot_general x3, matrix products, marg_terms(): jnp.einsum('sai,saj->aij', panel_cols.reshape(rows_total, block_count, bl...  27.1 us
    dot_general x1, matrix products, local(): jnp.dot(low_cov, panel_low, precision=HIGH, preferred_element_type=jnp.fl...  22.3 us
  transfers between devices with their start and end apart: 12, of which 9 were waited for; matrix products, arithmetic and copies ran while one was open for 22% of the time, Pallas kernels for 0%

commit v1 on v0

--- a/solution.py
+++ b/solution.py
@@ -1,9 +1,22 @@
+import functools
 import jax
 import jax.numpy as jnp
 from jax import lax
 from jax.sharding import PartitionSpec as P
 
 HIGH = lax.Precision.HIGHEST
+
+
+def place_the_waves(message, row_axis):
+    n_all = jax.lax.axis_size(row_axis)
+    passed = lambda then: [(k0, k0 ^ then) for k0 in range(n_all)]
+    lower = message
+    for q in range(n_all.bit_length() - 1):
+        lower = lower + jax.lax.ppermute(lower, axis_name=row_axis, perm=passed(1 << q))
+    return lower
+
+
+rest_the_cube = functools.partial(place_the_waves, row_axis="rows")
 
 
 def from_partner(value, axis, bit):
@@ -124,7 +137,7 @@
     partial_value = marg_terms(panel_rows, cross_top, block_size)
     piece_rows = partial_value.shape[0] // row_count
     own_diag = lax.dynamic_slice_in_dim(diag_top, rows_index * piece_rows, piece_rows, 0)
-    summed_terms = lax.psum(partial_value, "rows")
+    summed_terms = rest_the_cube(partial_value)
     marginal_top = own_diag - lax.dynamic_slice_in_dim(
         summed_terms, rows_index * piece_rows, piece_rows, 0
     )

time: 720 us -> 621 us (0.86)
  waiting for transfers between devices: 430 us -> 352 us
  matrix products: 143 us -> 126 us
    psum x1, waiting for transfers between devices: 54.4 us -> 0.02 us  [local(): summed = lax.psum((chosen_mid, chosen_mid_diag), 'rows')]
    ppermute x8, waiting for transfers between devices: 355 us -> 329 us  [from_partner(): lax.ppermute(value, axis, [(i, i ^ 1 << bit) for i in range(lax.axis_size...]
    all_gather x1, waiting for transfers between devices: 3.92 us -> 16 us  [local(): lax.all_gather(pieces[0], 'rows', axis=0, tiled=True)]
    all_gather x1, waiting for transfers between devices: 16.3 us -> 4.72 us  [local(): lax.all_gather(pieces[2], 'rows', axis=0, tiled=True)]
    dot_general x3, matrix products: 27.1 us -> 17 us  [marg_terms(): jnp.einsum('sai,saj->aij', panel_cols.reshape(rows_total, block_count, bl...]
    dot_general x2, matrix products: 43.3 us -> 34 us  [child_cov(): jnp.dot(parent_cov, chosen, precision=HIGH, preferred_element_type=jnp.fl...]
    unnamed x55 -> x43, local copies, waits for them, and re-layouts: 28.7 us -> 28.2 us
  transfers between devices with their start and end apart: 12 -> 14, of which waited for: 9 -> 9; matrix products, arithmetic and copies ran while one was open for 22% -> 20% of each run, Pallas kernels for 0% -> 0%
where the time goes in v1:
time: 621 us; the launch traced here: 615 us
  waiting for transfers between devices  352 us (57%)
  matrix products  126 us (20%)
  local copies, waits for them, and re-layouts  84.4 us (14%)
  other arithmetic  25.3 us (4%)
  between operations  14.4 us (2%)
  starting transfers between devices  12.6 us (2%)
    ppermute x8, waiting for transfers between devices, from_partner(): lax.ppermute(value, axis, [(i, i ^ 1 << bit) for i in range(lax.axis_size...  329 us
    dot_general x2, matrix products, child_cov(): jnp.dot(parent_cov, chosen, precision=HIGH, preferred_element_type=jnp.fl...  34 us
    dot_general x2, matrix products, child_cov(): jnp.dot(chosen.T, product, precision=HIGH, preferred_element_type=jnp.flo...  32.4 us
    gather x4, local copies, waits for them, and re-layouts, select_blocks(): jnp.take(panel_cols.reshape(rows_total, local_count, block_size), wanted,...  30 us
    unnamed x43, local copies, waits for them, and re-layouts  28.2 us
    dot_general x1, matrix products, local(): jnp.dot(low_cov, panel_low, precision=HIGH, preferred_element_type=jnp.fl...  22.5 us
    dot_general x3, matrix products, marg_terms(): jnp.einsum('sai,saj->aij', panel_cols.reshape(rows_total, block_count, bl...  17 us
    all_gather x1, waiting for transfers between devices, local(): lax.all_gather(pieces[0], 'rows', axis=0, tiled=True)  16 us
  transfers between devices with their start and end apart: 14, of which 9 were waited for; matrix products, arithmetic and copies ran while one was open for 20% of the time, Pallas kernels for 0%

profile of v1, /device:TPU:0, one launch (start us, length us, event | category | flops | bytes accessed | tf_op | source)
XLA Modules:
  0.0 614.8 jit_solution(3641425093928977869)
XLA Ops:
  8.8 3.5 copy.42
  14.7 4.3 gather_fusion.4
  19.0 9.2 %copy.46 = f32[1024,8,256]{0,2,1:T(8,128)} copy(f32[1024,8,256]{2,0,1:T(8,128)} %bitcast.67) | data formatting | bytes 16777216 | tf_op jit(solution)/shard_map/jit(_take)/gather | solution.py:38
  29.3 5.9 fusion
  38.5 3.1 collective-permute-start
  41.5 23.2 %collective-permute-done = f32[256,1024]{1,0:T(8,128)S(1)} collective-permute-done((f32[256,1024]{1,0:T(8,128)S(1)}, f32[256,1024]{1,0:T(8,128)S(1)}, u32[]{:S(2)}, u32[]{:S(2)}) %collective-permute-start) | collective-permute-done | bytes 1048608 | tf_op jit(solution)/shard_map/ppermute | solution.py:23
  66.7 22.6 %collective-permute-done.1 = f32[256,1024]{1,0:T(8,128)S(1)} collective-permute-done((f32[256,1024]{1,0:T(8,128)S(1)}, f32[256,1024]{1,0:T(8,128)S(1)}, u32[]{:S(2)}, u32[]{:S(2)}) %collective-permute-start.1) | collective-permute-done | bytes 1048608 | tf_op jit(solution)/shard_map/ppermute | solution.py:23
  91.3 6.6 %copy.39 = f32[1024,1536]{0,1:T(8,128)} copy(f32[1024,1536]{1,0:T(8,128)} %param.10) | data formatting | bytes 12582912 | tf_op args[1]
  97.9 6.7 %copy.40 = f32[1024,6,256]{2,0,1:T(8,128)} copy(f32[1024,6,256]{0,2,1:T(8,128)} %bitcast.73) | data formatting | bytes 12582912 | tf_op jit(solution)/shard_map/reshape | solution.py:38
  104.6 7.2 %gather_fusion.1 = f32[8,1024,256]{2,1,0:T(8,128)} fusion(f32[1024,6,256]{2,0,1:T(8,128)} %copy.40, s32[1024]{0:T(1024)S(1)} %pad_clamp_fusion.2), kind=kCustom, calls=%fused_computation.1 | custom fusion | bytes 16777248 | tf_op jit(solution)/shard_map/jit(_take)/gather | solution.py:38
  111.8 9.2 %copy.41 = f32[1024,8,256]{0,2,1:T(8,128)} copy(f32[1024,8,256]{2,0,1:T(8,128)} %bitcast.68) | data formatting | bytes 16777216 | tf_op jit(solution)/shard_map/jit(_take)/gather | solution.py:38
  128.9 53.2 %collective-permute-done.6 = f32[512,256]{1,0:T(8,128)S(1)} collective-permute-done((f32[512,256]{1,0:T(8,128)S(1)}, f32[512,256]{1,0:T(8,128)S(1)}, u32[]{:S(2)}, u32[]{:S(2)}) %collective-permute-start.6) | collective-permute-done | bytes 524320 | tf_op jit(solution)/shard_map/ppermute | solution.py:23
  183.5 10.7 %collective-permute-done.7 = f32[512,256]{1,0:T(8,128)S(1)} collective-permute-done((f32[512,256]{1,0:T(8,128)S(1)}, f32[512,256]{1,0:T(8,128)S(1)}, u32[]{:S(2)}, u32[]{:S(2)}) %collective-permute-start.7) | collective-permute-done | bytes 524320 | tf_op jit(solution)/shard_map/ppermute | solution.py:23
  199.3 43.9 %collective-permute-done.5 = f32[256,2048]{0,1:T(8,128)S(1)} collective-permute-done((f32[256,2048]{0,1:T(8,128)S(1)}, f32[256,2048]{0,1:T(8,128)S(1)}, u32[]{:S(2)}, u32[]{:S(2)}) %collective-permute-start.5) | collective-permute-done | bytes 2097184 | tf_op jit(solution)/shard_map/ppermute | solution.py:23
  247.4 16.0 %all-gather.4.cloned.1.call-done = f32[1024,1024]{1,0:T(8,128)} async-done(((f32[256,1024]{1,0:T(8,128)}), f32[1024,1024]{1,0:T(8,128)}) %all-gather.4.cloned.1.call-update) | async-done | bytes 4194320 | tf_op jit(solution)/shard_map/all_gather | solution.py:116
  263.5 7.9 %convolution_negate_fusion.1 = f32[256,1536]{1,0:T(8,128)S(1)} fusion(f32[1024,1536]{1,0:T(8,128)} %param.10, f32[1024,1024]{1,0:T(8,128)} %all-gather.4.cloned.1.call-done, s32[]{:T(128)S(6)} %select_n.181), kind=kOutput, calls=%fused_computation.15 | convolution fusion | flops 4832231424 | bytes 8912900 | tf_op jit(solution)/shard_map/dot_general | solution.py:135
  273.1 3.2 fusion.26
  280.5 6.6 %copy.48 = f32[1024,1536]{0,1:T(8,128)} copy(f32[1024,1536]{1,0:T(8,128)} %param.15) | data formatting | bytes 12582912 | tf_op args[6]
  287.1 4.7 all-gather.8.cloned.1.call-done
  293.1 175.8 %collective-permute-done.9 = f32[2048,256]{1,0:T(8,128)} collective-permute-done((f32[2048,256]{1,0:T(8,128)}, f32[2048,256]{1,0:T(8,128)}, u32[]{:S(2)}, u32[]{:S(2)}) %collective-permute-start.9) | collective-permute-done | bytes 2097184 | tf_op jit(solution)/shard_map/ppermute | solution.py:23
  472.2 3.0 copy.55
  475.2 3.0 copy.57
  480.2 17.3 %fusion.4 = f32[1024,1024]{1,0:T(8,128)S(1)} fusion(f32[1024,1024]{1,0:T(8,128)} %all-gather.4.cloned.1.call-done, f32[1024,2048]{0,1:T(8,128)} %all-gather.6.cloned.1.call-done, s32[]{:T(128)S(6)} %select_n.193), kind=kOutput, calls=%fused_computation.13 | convolution fusion | flops 12884901888 | bytes 12582916 | tf_op jit(solution)/shard_map/dot_general | solution.py:50
  497.5 16.1 %fusion.8 = f32[1024,1024]{1,0:T(8,128)S(1)} fusion(f32[1024,1024]{1,0:T(8,128)S(1)} %bitcast.76, f32[1024,1024]{1,0:T(8,128)S(1)} %fusion.4, f32[1024,2048]{0,1:T(8,128)} %all-gather.6.cloned.1.call-done, s32[]{:T(128)S(6)} %select_n.193), kind=kOutput, calls=%fused_computation.22 | convolution fusion | flops 12885950464 | bytes 16777220 | tf_op jit(solution)/shard_map/dot_general | solution.py:51
  513.7 12.2 %convolution_negate_fusion.2 = f32[1024,768]{0,1:T(8,128)} fusion(f32[1024,1024]{1,0:T(8,128)S(1)} %fusion.8, f32[1024,768]{1,0:T(8,128)S(1)} %copy-done.9), kind=kOutput, calls=%fused_computation.23 | convolution fusion | flops 9664462848 | bytes 10485760 | tf_op jit(solution)/shard_map/dot_general | solution.py:150
  525.9 16.7 %fusion.11 = f32[1024,1024]{1,0:T(8,128)S(1)} fusion(f32[1024,1024]{1,0:T(8,128)S(1)} %fusion.8, f32[1024,2048]{0,1:T(8,128)} %collective-permute-done.8, s32[]{:T(128)S(6)} %select_n.204, f32[1024,2048]{0,1:T(8,128)S(1)} %bitcast.82), kind=kOutput, calls=%fused_computation.25 | convolution fusion | flops 12885950464 | bytes 16777220 | tf_op jit(solution)/shard_map/dot_general | solution.py:50
  542.6 16.3 %fusion.12 = f32[1024,1024]{1,0:T(8,128)S(1)} fusion(f32[1024,1024]{1,0:T(8,128)S(1)} %fusion.11, f32[1024,2048]{0,1:T(8,128)} %collective-permute-done.8, s32[]{:T(128)S(6)} %select_n.204, f32[1024,2048]{0,1:T(8,128)S(1)} %bitcast.82), kind=kOutput, calls=%fused_computation.26 | convolution fusion | flops 12885950464 | bytes 16777220 | tf_op jit(solution)/shard_map/dot_general | solution.py:51
  558.9 22.5 %convolution_negate_fusion = f32[1024,1536]{1,0:T(8,128)} fusion(f32[1024,1536]{1,0:T(8,128)S(1)} %bitcast.84, f32[1024,1024]{1,0:T(8,128)S(1)} %fusion.12, f32[1024,1024]{1,0:T(8,128)S(1)} %bitcast.90), kind=kOutput, calls=%fused_computation.8 | convolution fusion | flops 19329974272 | bytes 20971520 | tf_op jit(solution)/shard_map/dot_general | solution.py:156
  581.5 6.6 %copy.47 = f32[1024,1536]{0,1:T(8,128)} copy(f32[1024,1536]{1,0:T(8,128)} %convolution_negate_fusion) | data formatting | bytes 12582912 | tf_op jit(solution)/shard_map/neg | solution.py:156
  588.0 3.8 copy.50
  591.9 5.3 fusion.27
  598.2 8.4 %fusion.28 = f32[6,256,256]{1,2,0:T(8,128)S(1)} fusion(f32[1024,6,256]{0,2,1:T(8,128)S(1)} %bitcast.72, f32[1024,6,256]{0,2,1:T(8,128)} %bitcast.71), kind=kOutput, calls=%fused_computation.80 | convolution fusion | flops 4831838208 | bytes 14155776 | tf_op jit(solution)/shard_map/sai,saj->aij/dot_general | solution.py:58
  (117 shorter events, 45.4 us)
Async XLA Ops:
  7.2 83.4 %copy-start = (s32[4,4]{1,0:T(4,128)S(1)}, s32[4,4]{1,0:T(4,128)}, u32[]{:S(2)}) copy-start(s32[4,4]{1,0:T(4,128)} %param.14) | copy-start | bytes 196
  7.2 237.7 %all-reduce.3.cloned.1.call-start = ((), (), s32[]{:S(2)}) async-start(), calls=%async_computation.3 | async-start | bytes 20971520 | tf_op jit(solution)/shard_map/psum | solution.py:129
  19.0 9.6 %copy-start.5 = (f32[768,256]{1,0:T(8,128)S(1)}, f32[768,256]{1,0:T(8,128)}, u32[]{:S(2)}) copy-start(f32[768,256]{1,0:T(8,128)} %param.13) | copy-start | bytes 2359300
  37.0 1.2 copy-start.11
  37.1 226.4 %all-gather.4.cloned.1.call-start = ((), (), s32[]{:S(2)}) async-start(), calls=%async_computation | async-start | bytes 5242880 | tf_op jit(solution)/shard_map/all_gather | solution.py:116
  38.5 26.2 %collective-permute-start = (f32[256,1024]{1,0:T(8,128)S(1)}, f32[256,1024]{1,0:T(8,128)S(1)}, u32[]{:S(2)}, u32[]{:S(2)}) collective-permute-start(f32[256,1024]{1,0:T(8,128)S(1)} %constant_dynamic-slice_fusion.2), channel_id=1, source_target_pairs={{0,4},{4,0},{8,12},{12,8},{16,20},{20,16},{24,28},{28,24},{1,5},{5... | collective-permute-start | bytes 3145736 | tf_op jit(solution)/shard_map/ppermute | solution.py:23
  64.9 24.5 %collective-permute-start.1 = (f32[256,1024]{1,0:T(8,128)S(1)}, f32[256,1024]{1,0:T(8,128)S(1)}, u32[]{:S(2)}, u32[]{:S(2)}) collective-permute-start(f32[256,1024]{1,0:T(8,128)S(1)} %fusion.45), channel_id=1, source_target_pairs={{0,8},{4,12},{8,0},{12,4},{16,24},{20,28},{24,16},{28,20},{1,9},{5... | collective-permute-start | bytes 3145736 | tf_op jit(solution)/shard_map/ppermute | solution.py:23
  90.5 201.3 %all-gather.8.cloned.1.call-start = ((), (), s32[]{:S(2)}) async-start(), calls=%async_computation.2 | async-start | bytes 2621440 | tf_op jit(solution)/shard_map/all_gather | solution.py:118
  124.3 71.4 %collective-permute-start.4 = (f32[256,2048]{0,1:T(8,128)}, f32[256,2048]{0,1:T(8,128)}, u32[]{:S(2)}, u32[]{:S(2)}) collective-permute-start(f32[256,2048]{0,1:T(8,128)} %fusion.6), channel_id=1, source_target_pairs={{0,4},{4,0},{8,12},{12,8},{16,20},{20,16},{24,28},{28,24},{1,5},{5... | collective-permute-start | bytes 6291464 | tf_op jit(solution)/shard_map/ppermute | solution.py:23
  128.2 53.9 %collective-permute-start.6 = (f32[512,256]{1,0:T(8,128)S(1)}, f32[512,256]{1,0:T(8,128)S(1)}, u32[]{:S(2)}, u32[]{:S(2)}) collective-permute-start(f32[512,256]{1,0:T(8,128)S(1)} %fusion.14), channel_id=1, source_target_pairs={{0,4},{4,0},{8,12},{12,8},{16,20},{20,16},{24,28},{28,24},{1,5},{5... | collective-permute-start | bytes 1572872 | tf_op jit(solution)/shard_map/ppermute | solution.py:23
  182.3 12.0 %collective-permute-start.7 = (f32[512,256]{1,0:T(8,128)S(1)}, f32[512,256]{1,0:T(8,128)S(1)}, u32[]{:S(2)}, u32[]{:S(2)}) collective-permute-start(f32[512,256]{1,0:T(8,128)S(1)} %fusion.44), channel_id=1, source_target_pairs={{0,8},{4,12},{8,0},{12,4},{16,24},{20,28},{24,16},{28,20},{1,9},{5... | collective-permute-start | bytes 1572872 | tf_op jit(solution)/shard_map/ppermute | solution.py:23
  195.1 285.1 %all-gather.6.cloned.1.call-start = ((), (), s32[]{:S(2)}) async-start(), calls=%async_computation.1 | async-start | bytes 10485760 | tf_op jit(solution)/shard_map/all_gather | solution.py:117
  198.4 44.8 %collective-permute-start.5 = (f32[256,2048]{0,1:T(8,128)S(1)}, f32[256,2048]{0,1:T(8,128)S(1)}, u32[]{:S(2)}, u32[]{:S(2)}) collective-permute-start(f32[256,2048]{0,1:T(8,128)S(1)} %fusion.43), channel_id=1, source_target_pairs={{0,8},{4,12},{8,0},{12,4},{16,24},{20,28},{24,16},{28,20},{1,9},{5... | collective-permute-start | bytes 6291464 | tf_op jit(solution)/shard_map/ppermute | solution.py:23
  244.9 281.0 %collective-permute-start.8 = (f32[1024,2048]{0,1:T(8,128)}, f32[1024,2048]{0,1:T(8,128)}, u32[]{:S(2)}, u32[]{:S(2)}) collective-permute-start(f32[1024,2048]{0,1:T(8,128)} %get-tuple-element.24), channel_id=1, source_target_pairs={{0,4},{4,0},{8,12},{12,8},{16,20},{20,16},{24,28},{28,24},{1,5},{5... | collective-permute-start | bytes 25165832 | tf_op jit(solution)/shard_map/ppermute | solution.py:23
  271.4 8.8 %copy-start.7 = (f32[256,1536]{1,0:T(8,128)}, f32[256,1536]{1,0:T(8,128)S(1)}, u32[]{:S(2)}) copy-start(f32[256,1536]{1,0:T(8,128)S(1)} %convolution_negate_fusion.1) | copy-start | bytes 4718596
  276.3 3.7 collective-permute-start.2
  276.7 192.2 %collective-permute-start.9 = (f32[2048,256]{1,0:T(8,128)}, f32[2048,256]{1,0:T(8,128)}, u32[]{:S(2)}, u32[]{:S(2)}) collective-permute-start(f32[2048,256]{1,0:T(8,128)} %get-tuple-element.25), channel_id=1, source_target_pairs={{0,4},{4,0},{8,12},{12,8},{16,20},{20,16},{24,28},{28,24},{1,5},{5... | collective-permute-start | bytes 6291464 | tf_op jit(solution)/shard_map/ppermute | solution.py:23
  280.2 198.0 %collective-permute-start.3 = (f32[1536,256]{1,0:T(8,128)S(1)}, f32[1536,256]{1,0:T(8,128)}, u32[]{:S(2)}, u32[]{:S(2)}) collective-permute-start(f32[1536,256]{1,0:T(8,128)S(1)} %bitcast_add_fusion), channel_id=1, source_target_pairs={{0,2},{1,3},{2,0},{3,1},{4,6},{5,7},{6,4},{7,5},{8,10},{9,11},{10,... | collective-permute-start | bytes 4718600 | tf_op jit(solution)/shard_map/ppermute | solution.py:15
  480.2 17.3 %copy-start.4 = (f32[128,8,4,256]{3,1,2,0:T(8,128)S(1)}, f32[128,8,4,256]{3,1,2,0:T(8,128)}, u32[]{:S(2)}) copy-start(f32[128,8,4,256]{3,1,2,0:T(8,128)} %copy.55) | copy-start | bytes 12582916
  480.2 45.7 %slice-start = ((s8[8388608]{0:T(1024)(128)(4,1)}), s8[4194304]{0:T(1024)(128)(4,1)S(1)}, s32[]{:S(2)}) async-start(s8[8388608]{0:T(1024)(128)(4,1)} %bitcast.81), calls=%async_computation.4 | async-start | bytes 8388608
  497.5 16.2 %copy-start.9 = (f32[1024,768]{1,0:T(8,128)S(1)}, f32[1024,768]{1,0:T(8,128)}, u32[]{:S(2)}) copy-start(f32[1024,768]{1,0:T(8,128)} %param.12) | copy-start | bytes 9437188
  497.5 28.3 %slice-start.1 = ((s8[8388608]{0:T(1024)(128)(4,1)}), s8[4194304]{0:T(1024)(128)(4,1)S(1)}, s32[]{:S(2)}) async-start(s8[8388608]{0:T(1024)(128)(4,1)} %bitcast.81), calls=%async_computation.5 | async-start | bytes 8388608
  525.9 33.0 %slice-start.2 = ((s8[6291456]{0:T(1024)(128)(4,1)}), s8[4194304]{0:T(1024)(128)(4,1)S(1)}, s32[]{:S(2)}) async-start(s8[6291456]{0:T(1024)(128)(4,1)} %bitcast.83), calls=%async_computation.6 | async-start | bytes 8388608
  542.6 16.3 %slice-start.3 = ((s8[6291456]{0:T(1024)(128)(4,1)}), s8[2097152]{0:T(1024)(128)(4,1)S(1)}, s32[]{:S(2)}) async-start(s8[6291456]{0:T(1024)(128)(4,1)} %bitcast.83), calls=%async_computation.7 | async-start | bytes 4194304
  542.6 16.3 %copy-start.8 = (f32[128,8,4,256]{3,1,2,0:T(8,128)S(1)}, f32[128,8,4,256]{3,1,2,0:T(8,128)}, u32[]{:S(2)}) copy-start(f32[128,8,4,256]{3,1,2,0:T(8,128)} %copy.57) | copy-start | bytes 12582916
  588.0 3.9 copy-start.2
  591.9 5.4 copy-start.6
  591.9 6.3 %copy-start.3 = (f32[1024,1536]{0,1:T(8,128)S(1)}, f32[1024,1536]{0,1:T(8,128)}, u32[]{:S(2)}) copy-start(f32[1024,1536]{0,1:T(8,128)} %copy.47) | copy-start | bytes 18874372
  598.2 8.5 %copy-start.10 = (f32[1536,256]{1,0:T(8,128)S(1)}, f32[1536,256]{1,0:T(8,128)}, u32[]{:S(2)}) copy-start(f32[1536,256]{1,0:T(8,128)} %param.16) | copy-start | bytes 4718596
  598.2 9.8 %copy-start.1 = (s32[4,4]{1,0:T(4,128)S(1)}, s32[4,4]{1,0:T(4,128)}, u32[]{:S(2)}) copy-start(s32[4,4]{1,0:T(4,128)} %param.14) | copy-start | bytes 196
Sparse Core Ops, SparseCore 0:
  37.2 189.4 all-reduce.2
  228.8 34.6 all-gather.3
  265.6 26.1 all-gather.7
  293.2 73.8 all-gather.5
